TPU v7x, 32 devices: a whole 2x2x4 slice. The times are simulated.
32 devices in a mesh: groups: 2 (over x), src: 8 (over z, y), rcv: 2 (over core).
Axes of the slice: x: 2, y: 2, z: 4, core: 2. Of those that a mesh axis runs over, the one named last changes fastest.
Arguments:
- spectra: bfloat16 [1280, 2, 2, 4096], P(('groups', 'src'), None, None, 'rcv'), parts along dimension 0, may hold values from -6 to 6
- pair_bins: int32 [1280, 80], P(('groups', 'src')), parts along dimension 0, may hold values from 0 to 15
- owners: int32 [32], P('groups'), parts along dimension 0, may hold values from 0 to 15, as said below
Outputs:
- bin_stacks: float32 [64, 2, 4096], P(('groups', 'src', 'rcv')), parts along dimension 0
There are 2 independent parts, one for each index of `groups`. A program takes and returns all parts, laid end to end along the dimension named above; each array names one. Nothing has to cross between parts.
Inputs may be any that keep to these rules, and one draw needn't show every extreme that they name: `owners`: each device owns at most 2 bins and some device owns exactly 2.
All inputs are finite; a program needn't handle non-finite values.
Results may differ from a plain program's by a relative error of at most 0.004.
Values may be sent and summed in bfloat16 or wider, within the bound.
A program may use at most 64 MiB of HBM per device.

v0:
```python
import math

import jax
import jax.numpy as jnp
from jax import lax
from jax.sharding import PartitionSpec as P

HALF = 32
CAP = 2


smooth_eps = 1e-06


def extended(block, sides, width):
    for axis, dim in sides:
        count = lax.axis_size(axis)
        forward = [(i, i + 1) for i in range(count - 1)]
        backward = [(target, source) for source, target in forward]
        low = lax.ppermute(
            lax.slice_in_dim(block, block.shape[dim] - width, None, axis=dim), axis, forward
        )
        high = lax.ppermute(lax.slice_in_dim(block, 0, width, axis=dim), axis, backward)
        block = jnp.concatenate([low, block, high], axis=dim)
    return block


def shifted(block, axis, distance):
    devices = range(lax.axis_size(axis))
    route = [(i - distance, i) for i in devices if i - distance in devices]
    return lax.ppermute(block, axis, route)


def box_smooth(padded, local, windows, width):
    tile = 128
    extra = jnp.pad(padded, ((0, 0), (0, 0), (0, tile - 2 * HALF)))
    head = extra[:, :, :width].reshape(-1, tile)
    tail = extra[:, :, tile : tile + width].reshape(-1, tile)
    row_ids = jnp.arange(2 * tile, dtype=jnp.int32)[:, None]
    col_ids = jnp.arange(tile, dtype=jnp.int32)[None, :]
    band = ((row_ids >= col_ids) & (row_ids <= col_ids + 2 * HALF)).astype(jnp.float32) / (
        2 * HALF + 1
    )
    result = jnp.dot(head, band[:tile], precision=lax.Precision.HIGHEST)
    result = result + jnp.dot(tail, band[tile:], precision=lax.Precision.HIGHEST)
    return result.reshape(local, windows, width)


def per_device(spectra, pair_bins, owners):
    width = spectra.shape[3]
    windows = spectra.shape[1]
    local = spectra.shape[0]
    nbins = owners.shape[0]
    nsrc = lax.axis_size("src")
    nrcv = lax.axis_size("rcv")
    ndev = nsrc * nrcv
    values = spectra.astype(jnp.float32)
    magnitude = jnp.sqrt(values[:, :, 0] ** 2 + values[:, :, 1] ** 2)
    padded = extended(magnitude, (("rcv", 2),), HALF)
    smooth = box_smooth(padded, local, windows, width)
    white = (values / (smooth[:, :, None, :] + smooth_eps)).astype(jnp.bfloat16)
    neighbour = shifted(white, "src", -1)
    src_index = lax.axis_index("src")
    valid = (src_index + 1 < nsrc).astype(jnp.float32)
    recv_re = neighbour[:, :, 0].astype(jnp.float32).transpose(1, 0, 2)
    recv_im = neighbour[:, :, 1].astype(jnp.float32).transpose(1, 0, 2)
    block = math.gcd(local, 8)
    turns = local // block
    own_re_all = white[:, :, 0].reshape(turns, block, windows, width).transpose(0, 2, 1, 3)
    own_im_all = white[:, :, 1].reshape(turns, block, windows, width).transpose(0, 2, 1, 3)
    labels = pair_bins.reshape(turns, block * local)
    bin_ids = jnp.arange(nbins, dtype=jnp.int32)

    def one_block(carry, inputs):
        own_re, own_im, label = inputs
        own_re = own_re.astype(jnp.float32)
        own_im = own_im.astype(jnp.float32)
        corr_re = jnp.zeros((block, local, width), jnp.float32)
        corr_im = jnp.zeros((block, local, width), jnp.float32)
        for window in range(windows):
            src_re = own_re[window][:, None, :]
            src_im = own_im[window][:, None, :]
            rec_re = recv_re[window][None]
            rec_im = recv_im[window][None]
            corr_re = corr_re + (src_re * rec_re + src_im * rec_im)
            corr_im = corr_im + (src_im * rec_re - src_re * rec_im)
        onehot = (label[None, :] == bin_ids[:, None]).astype(jnp.float32)
        added_re = jnp.dot(onehot, corr_re.reshape(-1, width), precision=lax.Precision.HIGHEST)
        added_im = jnp.dot(onehot, corr_im.reshape(-1, width), precision=lax.Precision.HIGHEST)
        return ((carry[0] + added_re, carry[1] + added_im), None)

    init = (jnp.zeros((nbins, width), jnp.float32), jnp.zeros((nbins, width), jnp.float32))
    (stack_re, stack_im), _ = lax.scan(one_block, init, (own_re_all, own_im_all, labels))
    stack = jnp.stack([stack_re, stack_im], axis=1) * valid
    counts = (
        jnp.sum((pair_bins.reshape(-1)[None, :] == bin_ids[:, None]).astype(jnp.float32), axis=1)
        * valid
    )
    same = owners[:, None] == owners[None, :]
    earlier = bin_ids[None, :] < bin_ids[:, None]
    slot = jnp.sum((same & earlier).astype(jnp.int32), axis=1)
    rows = owners * CAP + slot
    rcv_index = lax.axis_index("rcv")
    masked = jnp.where(rcv_index == 0, counts, 0.0)
    outgoing = (
        jnp.zeros((ndev * CAP, 2, width), jnp.float32)
        .at[rows]
        .set(stack)
        .reshape(ndev, CAP, 2, width)
    )
    out_counts = jnp.zeros((ndev * CAP,), jnp.float32).at[rows].set(masked).reshape(ndev, CAP)
    arrived, arrived_counts = (
        lax.all_to_all(outgoing, ("src", "rcv"), split_axis=0, concat_axis=0, tiled=True),
        lax.all_to_all(out_counts, ("src", "rcv"), split_axis=0, concat_axis=0, tiled=True),
    )
    summed = jnp.sum(arrived.reshape(nsrc, nrcv, CAP, 2, width), axis=0)
    sums = jnp.concatenate([summed[0], summed[1]], axis=2)
    total_counts = jnp.sum(arrived_counts, axis=0)
    return sums / jnp.sqrt(jnp.maximum(total_counts, 1.0))[:, None, None]


def solution(mesh):
    in_specs = (P(("groups", "src"), None, None, "rcv"), P(("groups", "src"), None), P("groups"))
    out_specs = P(("groups", "src", "rcv"), None, None)
    return jax.shard_map(
        per_device, mesh=mesh, in_specs=in_specs, out_specs=out_specs, check_vma=False
    )
```

profile of v0, /device:TPU:0, one launch (start us, length us, event | category | flops | bytes accessed | tf_op | source)
XLA Modules:
  0.0 216.3 jit_solution(6516945043682893194)
XLA Ops:
  26.7 8.9 %all-to-all-start.1 = ((f32[16,1,2]{2,1,0:T(1,128)}), f32[16,1,2]{2,1,0:T(1,128)S(1)}, u32[]{:S(2)}, u32[]{:S(2)}) async-start(f32[16,1,2]{2,1,0:T(1,128)} %bitcast.15), calls=%async_computation.1 | async-start | bytes 16384 | tf_op jit(solution)/shard_map/all_to_all | solution.py:114
  37.4 19.8 %collective-permute-done.2 = bf16[80,2,2,2048]{3,0,1,2:T(8,128)(2,1)} collective-permute-done((bf16[80,2,2,2048]{3,0,1,2:T(8,128)(2,1)S(1)}, bf16[80,2,2,2048]{3,0,1,2:T(8,128)(2,1)}, u32[]{:S(2)}, u32[]{:S(2)}) %collective-permute-start.2) | collective-permute-done | bytes 1310752 | tf_op jit(solution)/shard_map/ppermute | solution.py:31
  58.8 132.5 %while.13 = (s32[]{:T(128)}, f32[16,2048]{1,0:T(8,128)S(1)}, f32[16,2048]{1,0:T(8,128)S(1)}, s32[10,640]{1,0:T(8,128)}, bf16[10,2,8,2048]{3,2,1,0:T(8,128)(2,1)}...) while((s32[]{:T(128)}, f32[16,2048]{1,0:T(8,128)S(1)}, ...), condition=%wide.region_2.3_spmd.clone, body=%wide.region_1.2_spmd.clone.sunk | while | flops 521883648 | bytes 51521680 | solution.py:93
  59.9 5.1 %subtract_add_fusion.2 = (f32[8,80,2048]{2,1,0:T(8,128)}, f32[8,80,2048]{2,1,0:T(8,128)}) fusion(f32[80,2048]{1,0:T(8,128)S(1)} %get-tuple-element.185, f32[8,2048]{1,0:T(8,128)S(1)} %get-tuple-element.187, f32[80,2048]{1,0:T(8,128)S(1)} %get-tuple-element.188, f32[8,2048]{1,0:T(8,128)S(1)} %get-tuple-element.190, ...), kind=kLoop, calls=%fused_computation.3.clone.1 | loop fusion | flops 18350080 | bytes 13369344 | tf_op jit(solution)/shard_map/while/body/eval_jaxpr/add | solution.py:86
  65.8 4.4 %convolution_add_fusion.6 = f32[16,2048]{1,0:T(8,128)S(1)} fusion(f32[640,2048]{1,0:T(8,128)} %bitcast.70, f32[16,2048]{1,0:T(8,128)S(1)} %get-tuple-element.209, pred[]{:T(512)S(6)} %compare.4, s32[640]{0:T(1024)S(1)} %dynamic-slice_reduce_fusion.2), kind=kOutput, calls=%fused_computation.5.clone.1 | convolution fusion | flops 251734016 | bytes 5507585 | tf_op jit(solution)/shard_map/while/body/eval_jaxpr/dot_general | solution.py:89
  73.1 5.1 %subtract_add_fusion.2 = (f32[8,80,2048]{2,1,0:T(8,128)}, f32[8,80,2048]{2,1,0:T(8,128)}) fusion(f32[80,2048]{1,0:T(8,128)S(1)} %get-tuple-element.185, f32[8,2048]{1,0:T(8,128)S(1)} %get-tuple-element.187, f32[80,2048]{1,0:T(8,128)S(1)} %get-tuple-element.188, f32[8,2048]{1,0:T(8,128)S(1)} %get-tuple-element.190, ...), kind=kLoop, calls=%fused_computation.3.clone.1 | loop fusion | flops 18350080 | bytes 13369344 | tf_op jit(solution)/shard_map/while/body/eval_jaxpr/add | solution.py:86
  79.0 4.4 %convolution_add_fusion.6 = f32[16,2048]{1,0:T(8,128)S(1)} fusion(f32[640,2048]{1,0:T(8,128)} %bitcast.70, f32[16,2048]{1,0:T(8,128)S(1)} %get-tuple-element.209, pred[]{:T(512)S(6)} %compare.4, s32[640]{0:T(1024)S(1)} %dynamic-slice_reduce_fusion.2), kind=kOutput, calls=%fused_computation.5.clone.1 | convolution fusion | flops 251734016 | bytes 5507585 | tf_op jit(solution)/shard_map/while/body/eval_jaxpr/dot_general | solution.py:89
  86.4 5.1 %subtract_add_fusion.2 = (f32[8,80,2048]{2,1,0:T(8,128)}, f32[8,80,2048]{2,1,0:T(8,128)}) fusion(f32[80,2048]{1,0:T(8,128)S(1)} %get-tuple-element.185, f32[8,2048]{1,0:T(8,128)S(1)} %get-tuple-element.187, f32[80,2048]{1,0:T(8,128)S(1)} %get-tuple-element.188, f32[8,2048]{1,0:T(8,128)S(1)} %get-tuple-element.190, ...), kind=kLoop, calls=%fused_computation.3.clone.1 | loop fusion | flops 18350080 | bytes 13369344 | tf_op jit(solution)/shard_map/while/body/eval_jaxpr/add | solution.py:86
  92.3 4.4 %convolution_add_fusion.6 = f32[16,2048]{1,0:T(8,128)S(1)} fusion(f32[640,2048]{1,0:T(8,128)} %bitcast.70, f32[16,2048]{1,0:T(8,128)S(1)} %get-tuple-element.209, pred[]{:T(512)S(6)} %compare.4, s32[640]{0:T(1024)S(1)} %dynamic-slice_reduce_fusion.2), kind=kOutput, calls=%fused_computation.5.clone.1 | convolution fusion | flops 251734016 | bytes 5507585 | tf_op jit(solution)/shard_map/while/body/eval_jaxpr/dot_general | solution.py:89
  99.6 5.1 %subtract_add_fusion.2 = (f32[8,80,2048]{2,1,0:T(8,128)}, f32[8,80,2048]{2,1,0:T(8,128)}) fusion(f32[80,2048]{1,0:T(8,128)S(1)} %get-tuple-element.185, f32[8,2048]{1,0:T(8,128)S(1)} %get-tuple-element.187, f32[80,2048]{1,0:T(8,128)S(1)} %get-tuple-element.188, f32[8,2048]{1,0:T(8,128)S(1)} %get-tuple-element.190, ...), kind=kLoop, calls=%fused_computation.3.clone.1 | loop fusion | flops 18350080 | bytes 13369344 | tf_op jit(solution)/shard_map/while/body/eval_jaxpr/add | solution.py:86
  105.5 4.4 %convolution_add_fusion.6 = f32[16,2048]{1,0:T(8,128)S(1)} fusion(f32[640,2048]{1,0:T(8,128)} %bitcast.70, f32[16,2048]{1,0:T(8,128)S(1)} %get-tuple-element.209, pred[]{:T(512)S(6)} %compare.4, s32[640]{0:T(1024)S(1)} %dynamic-slice_reduce_fusion.2), kind=kOutput, calls=%fused_computation.5.clone.1 | convolution fusion | flops 251734016 | bytes 5507585 | tf_op jit(solution)/shard_map/while/body/eval_jaxpr/dot_general | solution.py:89
  112.9 5.1 %subtract_add_fusion.2 = (f32[8,80,2048]{2,1,0:T(8,128)}, f32[8,80,2048]{2,1,0:T(8,128)}) fusion(f32[80,2048]{1,0:T(8,128)S(1)} %get-tuple-element.185, f32[8,2048]{1,0:T(8,128)S(1)} %get-tuple-element.187, f32[80,2048]{1,0:T(8,128)S(1)} %get-tuple-element.188, f32[8,2048]{1,0:T(8,128)S(1)} %get-tuple-element.190, ...), kind=kLoop, calls=%fused_computation.3.clone.1 | loop fusion | flops 18350080 | bytes 13369344 | tf_op jit(solution)/shard_map/while/body/eval_jaxpr/add | solution.py:86
  126.1 5.1 %subtract_add_fusion.2 = (f32[8,80,2048]{2,1,0:T(8,128)}, f32[8,80,2048]{2,1,0:T(8,128)}) fusion(f32[80,2048]{1,0:T(8,128)S(1)} %get-tuple-element.185, f32[8,2048]{1,0:T(8,128)S(1)} %get-tuple-element.187, f32[80,2048]{1,0:T(8,128)S(1)} %get-tuple-element.188, f32[8,2048]{1,0:T(8,128)S(1)} %get-tuple-element.190, ...), kind=kLoop, calls=%fused_computation.3.clone.1 | loop fusion | flops 18350080 | bytes 13369344 | tf_op jit(solution)/shard_map/while/body/eval_jaxpr/add | solution.py:86
  132.0 4.4 %convolution_add_fusion.6 = f32[16,2048]{1,0:T(8,128)S(1)} fusion(f32[640,2048]{1,0:T(8,128)} %bitcast.70, f32[16,2048]{1,0:T(8,128)S(1)} %get-tuple-element.209, pred[]{:T(512)S(6)} %compare.4, s32[640]{0:T(1024)S(1)} %dynamic-slice_reduce_fusion.2), kind=kOutput, calls=%fused_computation.5.clone.1 | convolution fusion | flops 251734016 | bytes 5507585 | tf_op jit(solution)/shard_map/while/body/eval_jaxpr/dot_general | solution.py:89
  139.4 5.1 %subtract_add_fusion.2 = (f32[8,80,2048]{2,1,0:T(8,128)}, f32[8,80,2048]{2,1,0:T(8,128)}) fusion(f32[80,2048]{1,0:T(8,128)S(1)} %get-tuple-element.185, f32[8,2048]{1,0:T(8,128)S(1)} %get-tuple-element.187, f32[80,2048]{1,0:T(8,128)S(1)} %get-tuple-element.188, f32[8,2048]{1,0:T(8,128)S(1)} %get-tuple-element.190, ...), kind=kLoop, calls=%fused_computation.3.clone.1 | loop fusion | flops 18350080 | bytes 13369344 | tf_op jit(solution)/shard_map/while/body/eval_jaxpr/add | solution.py:86
  145.3 4.4 %convolution_add_fusion.6 = f32[16,2048]{1,0:T(8,128)S(1)} fusion(f32[640,2048]{1,0:T(8,128)} %bitcast.70, f32[16,2048]{1,0:T(8,128)S(1)} %get-tuple-element.209, pred[]{:T(512)S(6)} %compare.4, s32[640]{0:T(1024)S(1)} %dynamic-slice_reduce_fusion.2), kind=kOutput, calls=%fused_computation.5.clone.1 | convolution fusion | flops 251734016 | bytes 5507585 | tf_op jit(solution)/shard_map/while/body/eval_jaxpr/dot_general | solution.py:89
  152.6 5.1 %subtract_add_fusion.2 = (f32[8,80,2048]{2,1,0:T(8,128)}, f32[8,80,2048]{2,1,0:T(8,128)}) fusion(f32[80,2048]{1,0:T(8,128)S(1)} %get-tuple-element.185, f32[8,2048]{1,0:T(8,128)S(1)} %get-tuple-element.187, f32[80,2048]{1,0:T(8,128)S(1)} %get-tuple-element.188, f32[8,2048]{1,0:T(8,128)S(1)} %get-tuple-element.190, ...), kind=kLoop, calls=%fused_computation.3.clone.1 | loop fusion | flops 18350080 | bytes 13369344 | tf_op jit(solution)/shard_map/while/body/eval_jaxpr/add | solution.py:86
  158.5 4.4 %convolution_add_fusion.6 = f32[16,2048]{1,0:T(8,128)S(1)} fusion(f32[640,2048]{1,0:T(8,128)} %bitcast.70, f32[16,2048]{1,0:T(8,128)S(1)} %get-tuple-element.209, pred[]{:T(512)S(6)} %compare.4, s32[640]{0:T(1024)S(1)} %dynamic-slice_reduce_fusion.2), kind=kOutput, calls=%fused_computation.5.clone.1 | convolution fusion | flops 251734016 | bytes 5507585 | tf_op jit(solution)/shard_map/while/body/eval_jaxpr/dot_general | solution.py:89
  165.9 5.1 %subtract_add_fusion.2 = (f32[8,80,2048]{2,1,0:T(8,128)}, f32[8,80,2048]{2,1,0:T(8,128)}) fusion(f32[80,2048]{1,0:T(8,128)S(1)} %get-tuple-element.185, f32[8,2048]{1,0:T(8,128)S(1)} %get-tuple-element.187, f32[80,2048]{1,0:T(8,128)S(1)} %get-tuple-element.188, f32[8,2048]{1,0:T(8,128)S(1)} %get-tuple-element.190, ...), kind=kLoop, calls=%fused_computation.3.clone.1 | loop fusion | flops 18350080 | bytes 13369344 | tf_op jit(solution)/shard_map/while/body/eval_jaxpr/add | solution.py:86
  171.8 4.4 %convolution_add_fusion.6 = f32[16,2048]{1,0:T(8,128)S(1)} fusion(f32[640,2048]{1,0:T(8,128)} %bitcast.70, f32[16,2048]{1,0:T(8,128)S(1)} %get-tuple-element.209, pred[]{:T(512)S(6)} %compare.4, s32[640]{0:T(1024)S(1)} %dynamic-slice_reduce_fusion.2), kind=kOutput, calls=%fused_computation.5.clone.1 | convolution fusion | flops 251734016 | bytes 5507585 | tf_op jit(solution)/shard_map/while/body/eval_jaxpr/dot_general | solution.py:89
  179.1 5.1 %subtract_add_fusion.2 = (f32[8,80,2048]{2,1,0:T(8,128)}, f32[8,80,2048]{2,1,0:T(8,128)}) fusion(f32[80,2048]{1,0:T(8,128)S(1)} %get-tuple-element.185, f32[8,2048]{1,0:T(8,128)S(1)} %get-tuple-element.187, f32[80,2048]{1,0:T(8,128)S(1)} %get-tuple-element.188, f32[8,2048]{1,0:T(8,128)S(1)} %get-tuple-element.190, ...), kind=kLoop, calls=%fused_computation.3.clone.1 | loop fusion | flops 18350080 | bytes 13369344 | tf_op jit(solution)/shard_map/while/body/eval_jaxpr/add | solution.py:86
  185.0 4.4 %convolution_add_fusion.6 = f32[16,2048]{1,0:T(8,128)S(1)} fusion(f32[640,2048]{1,0:T(8,128)} %bitcast.70, f32[16,2048]{1,0:T(8,128)S(1)} %get-tuple-element.209, pred[]{:T(512)S(6)} %compare.4, s32[640]{0:T(1024)S(1)} %dynamic-slice_reduce_fusion.2), kind=kOutput, calls=%fused_computation.5.clone.1 | convolution fusion | flops 251734016 | bytes 5507585 | tf_op jit(solution)/shard_map/while/body/eval_jaxpr/dot_general | solution.py:89
  195.0 6.0 %all-to-all-start = ((f32[16,2,2,2048]{3,2,1,0:T(2,128)}), f32[16,2,2,2048]{3,2,1,0:T(2,128)S(1)}, u32[]{:S(2)}, u32[]{:S(2)}) async-start(f32[16,2,2,2048]{3,2,1,0:T(2,128)} %bitcast.11), calls=%async_computation | async-start | bytes 1048576 | tf_op jit(solution)/shard_map/all_to_all | solution.py:113
  201.1 14.2 %all-to-all-done = f32[16,2,2,2048]{3,2,1,0:T(2,128)S(1)} async-done(((f32[16,2,2,2048]{3,2,1,0:T(2,128)}), f32[16,2,2,2048]{3,2,1,0:T(2,128)S(1)}, u32[]{:S(2)}, u32[]{:S(2)}) %all-to-all-start) | async-done | bytes 524320 | tf_op jit(solution)/shard_map/all_to_all | solution.py:113
  (132 shorter events, 75.3 us)
Async XLA Ops:
  2.1 4.3 %copy-start.2 = (s32[80,80]{1,0:T(8,128)S(1)}, s32[80,80]{1,0:T(8,128)}, u32[]{:S(2)}) copy-start(s32[80,80]{1,0:T(8,128)} %param.6) | copy-start | bytes 76804
  2.6 4.1 %collective-permute-start = (f32[80,2,32]{2,0,1:T(8,128)S(1)}, f32[80,2,32]{2,0,1:T(8,128)S(1)}, u32[]{:S(2)}, u32[]{:S(2)}) collective-permute-start(f32[80,2,32]{2,0,1:T(8,128)S(1)} %get-tuple-element.119), channel_id=1, source_target_pairs={{0,1},{2,3},{4,5},{6,7},{8,9},{10,11},{12,13},{14,15},{16,17},{18,... | collective-permute-start | bytes 61448 | tf_op jit(solution)/shard_map/ppermute | solution.py:20
  5.0 3.2 %collective-permute-start.1 = (f32[80,2,32]{2,0,1:T(8,128)S(1)}, f32[80,2,32]{2,0,1:T(8,128)S(1)}, u32[]{:S(2)}, u32[]{:S(2)}) collective-permute-start(f32[80,2,32]{2,0,1:T(8,128)S(1)} %get-tuple-element.118), channel_id=1, source_target_pairs={{1,0},{3,2},{5,4},{7,6},{9,8},{11,10},{13,12},{15,14},{17,16},{19,... | collective-permute-start | bytes 61448 | tf_op jit(solution)/shard_map/ppermute | solution.py:23
  21.6 1.3 copy-start.1
  22.9 2.1 copy-start.3
  23.7 33.5 %collective-permute-start.2 = (bf16[80,2,2,2048]{3,0,1,2:T(8,128)(2,1)S(1)}, bf16[80,2,2,2048]{3,0,1,2:T(8,128)(2,1)}, u32[]{:S(2)}, u32[]{:S(2)}) collective-permute-start(bf16[80,2,2,2048]{3,0,1,2:T(8,128)(2,1)S(1)} %divide_convert_fusion), channel_id=1, source_target_pairs={{2,0},{4,2},{6,4},{8,6},{10,8},{12,10},{14,12},{3,1},{5,3},{7,5},{... | collective-permute-start | bytes 3932168 | tf_op jit(solution)/shard_map/ppermute | solution.py:31
  26.7 168.3 %all-to-all-start.1 = ((f32[16,1,2]{2,1,0:T(1,128)}), f32[16,1,2]{2,1,0:T(1,128)S(1)}, u32[]{:S(2)}, u32[]{:S(2)}) async-start(f32[16,1,2]{2,1,0:T(1,128)} %bitcast.15), calls=%async_computation.1 | async-start | bytes 16384 | tf_op jit(solution)/shard_map/all_to_all | solution.py:114
  65.8 4.4 %copy-start = (f32[8,80,2048]{2,1,0:T(8,128)S(1)}, f32[8,80,2048]{2,1,0:T(8,128)}, u32[]{:S(2)}) copy-start(f32[8,80,2048]{2,1,0:T(8,128)} %get-tuple-element.195) | copy-start | bytes 15728644 | tf_op jit(solution)/shard_map/while
  79.0 4.4 %copy-start = (f32[8,80,2048]{2,1,0:T(8,128)S(1)}, f32[8,80,2048]{2,1,0:T(8,128)}, u32[]{:S(2)}) copy-start(f32[8,80,2048]{2,1,0:T(8,128)} %get-tuple-element.195) | copy-start | bytes 15728644 | tf_op jit(solution)/shard_map/while
  92.3 4.4 %copy-start = (f32[8,80,2048]{2,1,0:T(8,128)S(1)}, f32[8,80,2048]{2,1,0:T(8,128)}, u32[]{:S(2)}) copy-start(f32[8,80,2048]{2,1,0:T(8,128)} %get-tuple-element.195) | copy-start | bytes 15728644 | tf_op jit(solution)/shard_map/while
  105.5 4.4 %copy-start = (f32[8,80,2048]{2,1,0:T(8,128)S(1)}, f32[8,80,2048]{2,1,0:T(8,128)}, u32[]{:S(2)}) copy-start(f32[8,80,2048]{2,1,0:T(8,128)} %get-tuple-element.195) | copy-start | bytes 15728644 | tf_op jit(solution)/shard_map/while
  118.7 4.4 %copy-start = (f32[8,80,2048]{2,1,0:T(8,128)S(1)}, f32[8,80,2048]{2,1,0:T(8,128)}, u32[]{:S(2)}) copy-start(f32[8,80,2048]{2,1,0:T(8,128)} %get-tuple-element.195) | copy-start | bytes 15728644 | tf_op jit(solution)/shard_map/while
  132.0 4.4 %copy-start = (f32[8,80,2048]{2,1,0:T(8,128)S(1)}, f32[8,80,2048]{2,1,0:T(8,128)}, u32[]{:S(2)}) copy-start(f32[8,80,2048]{2,1,0:T(8,128)} %get-tuple-element.195) | copy-start | bytes 15728644 | tf_op jit(solution)/shard_map/while
  145.2 4.4 %copy-start = (f32[8,80,2048]{2,1,0:T(8,128)S(1)}, f32[8,80,2048]{2,1,0:T(8,128)}, u32[]{:S(2)}) copy-start(f32[8,80,2048]{2,1,0:T(8,128)} %get-tuple-element.195) | copy-start | bytes 15728644 | tf_op jit(solution)/shard_map/while
  158.5 4.4 %copy-start = (f32[8,80,2048]{2,1,0:T(8,128)S(1)}, f32[8,80,2048]{2,1,0:T(8,128)}, u32[]{:S(2)}) copy-start(f32[8,80,2048]{2,1,0:T(8,128)} %get-tuple-element.195) | copy-start | bytes 15728644 | tf_op jit(solution)/shard_map/while
  171.7 4.4 %copy-start = (f32[8,80,2048]{2,1,0:T(8,128)S(1)}, f32[8,80,2048]{2,1,0:T(8,128)}, u32[]{:S(2)}) copy-start(f32[8,80,2048]{2,1,0:T(8,128)} %get-tuple-element.195) | copy-start | bytes 15728644 | tf_op jit(solution)/shard_map/while
  185.0 4.4 %copy-start = (f32[8,80,2048]{2,1,0:T(8,128)S(1)}, f32[8,80,2048]{2,1,0:T(8,128)}, u32[]{:S(2)}) copy-start(f32[8,80,2048]{2,1,0:T(8,128)} %get-tuple-element.195) | copy-start | bytes 15728644 | tf_op jit(solution)/shard_map/while
  195.0 20.3 %all-to-all-start = ((f32[16,2,2,2048]{3,2,1,0:T(2,128)}), f32[16,2,2,2048]{3,2,1,0:T(2,128)S(1)}, u32[]{:S(2)}, u32[]{:S(2)}) async-start(f32[16,2,2,2048]{3,2,1,0:T(2,128)} %bitcast.11), calls=%async_computation | async-start | bytes 1048576 | tf_op jit(solution)/shard_map/all_to_all | solution.py:113
where the time goes:
time: 218 us; the launch traced here: 216 us
  other arithmetic  66.6 us (31%)
  matrix products  65.1 us (30%)
  waiting for transfers between devices  35.6 us (16%)
  local copies, waits for them, and re-layouts  28.4 us (13%)
  starting transfers between devices  20 us (9%)
    add x10, other arithmetic, one_block(): corr_im = corr_im + (src_im * rec_re - src_re * rec_im)  51.3 us
    dot_general x10, matrix products, one_block(): jnp.dot(onehot, corr_im.reshape(-1, width), precision=lax.Precision.HIGHEST)  44.3 us
    ppermute x1, waiting for transfers between devices, shifted(): return lax.ppermute(block, axis, route)  19.8 us
    dot_general x10, matrix products, one_block(): jnp.dot(onehot, corr_re.reshape(-1, width), precision=lax.Precision.HIGHEST)  18.4 us
    all_to_all x1, waiting for transfers between devices, per_device(): lax.all_to_all(outgoing, ('src', 'rcv'), split_axis=0, concat_axis=0, til...  14.2 us
    all_to_all x1, starting transfers between devices, per_device(): lax.all_to_all(out_counts, ('src', 'rcv'), split_axis=0, concat_axis=0, t...  8.93 us
    convert_element_type x10, other arithmetic, one_block(): own_im = own_im.astype(jnp.float32)  8.59 us
    dynamic_slice x10, local copies, waits for them, and re-layouts, per_device(): lax.scan(one_block, init, (own_re_all, own_im_all, labels))  7.42 us
  transfers between devices with their start and end apart: 5, of which 3 were waited for; matrix products, arithmetic and copies ran while one was open for 65% of the time, Pallas kernels for 0%

commit v1 on v0

v1 whole, which is shorter than its diff:
```python
import functools

import jax
import jax.numpy as jnp
from jax import lax
from jax.experimental import pallas as pl
from jax.experimental.pallas import tpu as pltpu
from jax.sharding import PartitionSpec as P

HALF = 32
CAP = 2
EDGE = 128
CHUNK = 256
smooth_eps = 1e-06
MESH = pl.DeviceIdType.MESH


def kernel(
    dims,
    x_ref,
    lab_ref,
    labt_ref,
    rows_ref,
    tiled_ref,
    out_ref,
    white,
    near,
    far,
    halo,
    mag_hi,
    mag_lo,
    band,
    onehot,
    own,
    prod,
    acc,
    send_part,
    recv_part,
    lab_in,
    count_out,
    count_in,
    near_send,
    near_recv,
    far_send,
    far_recv,
    halo_sems,
    lab_sems,
    count_send,
    count_recv,
    part_send,
    part_recv,
):
    nsrc, nrcv, nbins, local, windows, chunks, group = dims
    half = chunks // 2
    width = chunks * CHUNK
    ndev = nsrc * nrcv
    s = lax.axis_index("src")
    r = lax.axis_index("rcv")
    me = s * nrcv + r
    par = lax.rem(s, 2)
    f32 = jnp.float32

    barrier = pltpu.get_barrier_semaphore()

    def greet(k, carry):
        o = lax.rem(me + k, ndev)
        pl.semaphore_signal(
            barrier,
            inc=1,
            device_id={"src": o // nrcv, "rcv": lax.rem(o, nrcv)},
            device_id_type=MESH,
        )
        return carry

    lax.fori_loop(1, ndev, greet, 0)

    def place(h, t):
        return h * half + r * (half - 1) + t * (1 - 2 * r)

    def put_magnitude(re, im, row, at, size):
        re = re.astype(f32)
        im = im.astype(f32)
        m = jnp.sqrt(re * re + im * im)
        hi = m.astype(jnp.bfloat16)
        mag_hi[pl.ds(row, local), pl.ds(at, size)] = hi
        mag_lo[pl.ds(row, local), pl.ds(at, size)] = (m - hi.astype(f32)).astype(jnp.bfloat16)

    zero = jnp.zeros((windows * local, EDGE), jnp.bfloat16)
    for buffer in (mag_hi, mag_lo):
        buffer[:, :EDGE] = zero
        buffer[:, EDGE + width :] = zero

    def magnitudes(j, carry):
        for w in range(windows):
            put_magnitude(
                x_ref[j, 2 * w],
                x_ref[j, 2 * w + 1],
                w * local,
                pl.multiple_of(EDGE + j * CHUNK, 128),
                CHUNK,
            )
        return carry

    lax.fori_loop(0, chunks, magnitudes, 0)
    tall = CHUNK + 2 * EDGE
    k_ids = lax.broadcasted_iota(jnp.int32, (tall, CHUNK), 0) - EDGE
    n_ids = lax.broadcasted_iota(jnp.int32, (tall, CHUNK), 1)
    band[...] = jnp.where((k_ids >= n_ids - HALF) & (k_ids <= n_ids + HALF), 1.0, 0.0).astype(
        jnp.bfloat16
    )

    def whiten(j):
        span = pl.ds(pl.multiple_of(j * CHUNK, 128), tall)
        total = jnp.dot(mag_hi[:, span], band[...], preferred_element_type=f32)
        total = total + jnp.dot(mag_lo[:, span], band[...], preferred_element_type=f32)
        inverse = 1.0 / (total / (2 * HALF + 1) + smooth_eps)
        for w in range(windows):
            part = inverse[w * local : (w + 1) * local]
            for p in range(2):
                white[j, 2 * w + p] = (x_ref[j, 2 * w + p].astype(f32) * part).astype(jnp.bfloat16)

    partner = s + 1 - 2 * par
    beyond = s + 2 - 4 * par
    sends_far = (beyond >= 0) & (beyond < nsrc)
    back = s - 2 + 4 * par
    has_far = (back >= 0) & (back < nsrc)

    def near_copy(t):
        return pltpu.make_async_remote_copy(
            src_ref=white.at[place(1 - par, t)],
            dst_ref=near.at[t],
            send_sem=near_send.at[t],
            recv_sem=near_recv.at[t],
            device_id={"src": partner},
            device_id_type=MESH,
        )

    def far_copy(t):
        return pltpu.make_async_remote_copy(
            src_ref=near.at[t],
            dst_ref=far.at[t],
            send_sem=far_send.at[t],
            recv_sem=far_recv.at[t],
            device_id={"src": beyond},
            device_id_type=MESH,
        )

    halo_copy = pltpu.make_async_remote_copy(
        src_ref=x_ref.at[
            (1 - r) * (chunks - 1), :, :, pl.ds(pl.multiple_of((1 - r) * (CHUNK - EDGE), 128), EDGE)
        ],
        dst_ref=halo,
        send_sem=halo_sems.at[0],
        recv_sem=halo_sems.at[1],
        device_id={"rcv": 1 - r},
        device_id_type=MESH,
    )
    lab_copy = pltpu.make_async_remote_copy(
        src_ref=labt_ref,
        dst_ref=lab_in,
        send_sem=lab_sems.at[0],
        recv_sem=lab_sems.at[1],
        device_id={"src": s + 1},
        device_id_type=MESH,
    )

    whiten(place(1 - par, 0))
    pl.semaphore_wait(barrier, ndev - 1)
    halo_copy.start()
    near_copy(0).start()

    @pl.when(s + 1 < nsrc)
    def _():
        lab_copy.start()

    def send_next(t, carry):
        whiten(place(1 - par, t))
        near_copy(t).start()
        return carry

    lax.fori_loop(1, half - 1, send_next, 0)
    halo_copy.wait_recv()
    for w in range(windows):
        put_magnitude(
            halo[2 * w],
            halo[2 * w + 1],
            w * local,
            pl.multiple_of((1 - r) * (EDGE + width), 128),
            EDGE,
        )
    whiten(place(1 - par, half - 1))
    near_copy(half - 1).start()

    labels = lab_ref[...]
    lanes = count_out.shape[1]
    lane_ids = lax.broadcasted_iota(jnp.int32, (8, lanes), 1)
    valid = (s + 1 < nsrc).astype(f32)

    def expand(b, counted):
        hits = jnp.where(labels == b, 1.0, 0.0).astype(f32)
        onehot[0, pl.ds(pl.multiple_of(b * local, 16), local), :] = hits.astype(jnp.bfloat16)
        found = jnp.sum(jnp.sum(hits, axis=0, keepdims=True), axis=1, keepdims=True)
        return counted + jnp.where(lane_ids == b, found, 0.0)

    counted = lax.fori_loop(0, nbins, expand, jnp.zeros((8, lanes), f32)) * valid
    count_out[...] = counted
    count_in[s] = counted

    def count_copy(o, slot):
        return pltpu.make_async_remote_copy(
            src_ref=count_out,
            dst_ref=count_in.at[slot],
            send_sem=count_send.at[o],
            recv_sem=count_recv.at[slot],
            device_id={"src": o},
            device_id_type=MESH,
        )

    def send_count(k, carry):
        count_copy(lax.rem(s + k, nsrc), s).start()
        return carry

    lax.fori_loop(1, nsrc, send_count, 0)

    def keep(t, carry):
        whiten(place(par, t))
        return carry

    lax.fori_loop(0, half, keep, 0)

    @pl.when(s > 0)
    def _():
        lab_copy.wait_recv()
        previous = lab_in[...]

        def expand_previous(b, carry):
            onehot[1, pl.ds(pl.multiple_of(b * local, 16), local), :] = jnp.where(
                previous == b, 1.0, 0.0
            ).astype(jnp.bfloat16)
            return carry

        lax.fori_loop(0, nbins, expand_previous, 0)

    def correlate(which, other, t, first):
        for k in range(2 * windows):
            own[k] = white[place(par, t), k].astype(f32)
        sign = (1 - 2 * which).astype(f32)
        rows = group * local

        def some(g, carry):
            picked = onehot[which, pl.ds(pl.multiple_of(g * rows, 16), rows), :]
            for k in range(2 * windows):
                prod[k] = jnp.dot(picked, other[t, k], preferred_element_type=f32)
            res, ims = [], []
            for b in range(group):
                at = slice(b * local, (b + 1) * local)
                re = jnp.zeros((local, CHUNK), f32)
                im = jnp.zeros((local, CHUNK), f32)
                for w in range(windows):
                    p_re, p_im = prod[2 * w, at], prod[2 * w + 1, at]
                    o_re, o_im = own[2 * w], own[2 * w + 1]
                    re = re + (o_re * p_re + o_im * p_im)
                    im = im + (o_im * p_re - o_re * p_im)
                res.append(jnp.sum(re, axis=0, keepdims=True))
                ims.append(jnp.sum(im, axis=0, keepdims=True))
            at = pl.ds(pl.multiple_of(g * group, group), group)
            re = jnp.concatenate(res, axis=0)
            im = jnp.concatenate(ims, axis=0) * sign
            if first:
                acc[t, 0, at] = re
                acc[t, 1, at] = im
            else:
                acc[t, 0, at] += re
                acc[t, 1, at] += im
            return carry

        lax.fori_loop(0, nbins // group, some, 0)

    def near_turn(t, carry):
        near_copy(t).wait_recv()

        @pl.when(sends_far)
        def _():
            far_copy(t).start()

        correlate(par, near, t, True)
        return carry

    def far_turn(t, carry):
        far_copy(t).wait_recv()
        correlate(1 - par, far, t, False)
        return carry

    def turn(t, carry):
        near_turn(t, 0)

        @pl.when((t > 0) & has_far)
        def _():
            far_turn(t - 1, 0)

        return carry

    lax.fori_loop(0, half, turn, 0)

    @pl.when(has_far)
    def _():
        far_turn(half - 1, 0)

    lines = CAP * 2 * half
    cols = half * 2 * nbins
    stacked = acc[...].reshape(cols, CHUNK).astype(jnp.bfloat16)
    batch = 16
    row_ids = lax.broadcasted_iota(jnp.int32, (batch * lines, cols), 0)
    col_ids = lax.broadcasted_iota(jnp.int32, (batch * lines, cols), 1)
    row_line = lax.rem(row_ids, 2 * half)
    col_turn = col_ids // (2 * nbins)
    col_line = lax.rem(col_ids // nbins, 2) * half + r * (half - 1) + col_turn * (1 - 2 * r)
    same_line = row_line == col_line
    row_slot = row_ids // (2 * half)

    def route(g, carry):
        pick = same_line & (tiled_ref[...] == row_slot + g * (batch * CAP))
        at = pl.ds(pl.multiple_of(g * (batch * lines), 16), batch * lines)
        pick = jnp.where(pick, 1.0, 0.0).astype(jnp.bfloat16)
        send_part[at] = jnp.dot(pick, stacked, preferred_element_type=f32).astype(jnp.bfloat16)
        return carry

    lax.fori_loop(0, ndev // batch, route, 0)

    def part_copy(o, slot):
        return pltpu.make_async_remote_copy(
            src_ref=send_part.at[pl.ds(pl.multiple_of(o * lines, 16), lines)],
            dst_ref=recv_part.at[slot],
            send_sem=part_send.at[o],
            recv_sem=part_recv.at[slot],
            device_id={"src": o // nrcv, "rcv": lax.rem(o, nrcv)},
            device_id_type=MESH,
        )

    def send_one(k, carry):
        part_copy(lax.rem(me + k, ndev), me).start()
        return carry

    lax.fori_loop(1, ndev, send_one, 0)
    recv_part[me] = send_part[pl.ds(pl.multiple_of(me * lines, 16), lines)]

    def take_count(k, carry):
        o = lax.rem(s + k, nsrc)
        count_copy(o, o).wait_recv()
        return carry

    lax.fori_loop(1, nsrc, take_count, 0)
    counts = jnp.sum(count_in[...], axis=0)[0:1]
    mine = [
        jnp.sum(jnp.where(rows_ref[...] == me * CAP + c, counts, 0.0), axis=1, keepdims=True)
        for c in range(CAP)
    ]
    line_ids = lax.broadcasted_iota(jnp.int32, (lines, 1), 0) // (2 * half)
    norm = jnp.zeros((lines, 1), f32)
    for c in range(CAP):
        norm = jnp.where(line_ids == c, jnp.sqrt(jnp.maximum(mine[c], 1.0)), norm)

    def take_part(k, carry):
        o = lax.rem(me + k, ndev)
        part_copy(o, o).wait_recv()
        return carry

    lax.fori_loop(1, ndev, take_part, 0)
    for rr in range(nrcv):
        for pp in range(2):

            def add(z, total):
                return total + recv_part[(2 * z + pp) * nrcv + rr].astype(f32)

            total = lax.fori_loop(0, nsrc // 2, add, jnp.zeros((lines, CHUNK), f32))
            out_ref[rr * 2 + pp] = total / norm

    for t in range(half):
        near_copy(t).wait_send()

    @pl.when(sends_far)
    def _():
        for t in range(half):
            far_copy(t).wait_send()

    halo_copy.wait_send()

    @pl.when(s + 1 < nsrc)
    def _():
        lab_copy.wait_send()

    def end_count(k, carry):
        count_copy(lax.rem(s + k, nsrc), s).wait_send()
        return carry

    lax.fori_loop(1, nsrc, end_count, 0)

    def end_part(k, carry):
        part_copy(lax.rem(me + k, ndev), me).wait_send()
        return carry

    lax.fori_loop(1, ndev, end_part, 0)


def per_device(spectra, pair_bins, owners):
    local, windows, _, width = spectra.shape
    nbins = owners.shape[0]
    nsrc = lax.axis_size("src")
    nrcv = lax.axis_size("rcv")
    ndev = nsrc * nrcv
    chunks = width // CHUNK
    half = chunks // 2
    lines = CAP * 2 * half
    lanes = -(-nbins // 128) * 128
    group = 8
    x = spectra.reshape(local, windows * 2, chunks, CHUNK).transpose(2, 1, 0, 3)
    bin_ids = jnp.arange(nbins, dtype=jnp.int32)
    same = owners[:, None] == owners[None, :]
    earlier = bin_ids[None, :] < bin_ids[:, None]
    rows = owners * CAP + jnp.sum((same & earlier).astype(jnp.int32), axis=1)
    rows_row = jnp.pad(rows, (0, lanes - nbins), constant_values=-1)[None]
    tiled = jnp.tile(rows, 2 * half)[None]
    dims = (nsrc, nrcv, nbins, local, windows, chunks, group)
    bf16, f32 = jnp.bfloat16, jnp.float32
    dma = pltpu.SemaphoreType.DMA
    vmem = pl.BlockSpec(memory_space=pltpu.VMEM)
    out = pl.pallas_call(
        functools.partial(kernel, dims),
        out_shape=jax.ShapeDtypeStruct((2 * nrcv, lines, CHUNK), f32),
        in_specs=[vmem] * 5,
        out_specs=vmem,
        scratch_shapes=[
            pltpu.VMEM((chunks, 2 * windows, local, CHUNK), bf16),
            pltpu.VMEM((half, 2 * windows, local, CHUNK), bf16),
            pltpu.VMEM((half, 2 * windows, local, CHUNK), bf16),
            pltpu.VMEM((2 * windows, local, EDGE), bf16),
            pltpu.VMEM((windows * local, width + 2 * EDGE), bf16),
            pltpu.VMEM((windows * local, width + 2 * EDGE), bf16),
            pltpu.VMEM((CHUNK + 2 * EDGE, CHUNK), bf16),
            pltpu.VMEM((2, nbins * local, local), bf16),
            pltpu.VMEM((2 * windows, local, CHUNK), f32),
            pltpu.VMEM((2 * windows, group * local, CHUNK), f32),
            pltpu.VMEM((half, 2, nbins, CHUNK), f32),
            pltpu.VMEM((ndev * lines, CHUNK), bf16),
            pltpu.VMEM((ndev, lines, CHUNK), bf16),
            pltpu.VMEM((local, local), jnp.int32),
            pltpu.VMEM((8, lanes), f32),
            pltpu.VMEM((nsrc, 8, lanes), f32),
            dma((half,)),
            dma((half,)),
            dma((half,)),
            dma((half,)),
            dma((2,)),
            dma((2,)),
            dma((nsrc,)),
            dma((nsrc,)),
            dma((ndev,)),
            dma((ndev,)),
        ],
        compiler_params=pltpu.CompilerParams(
            collective_id=0, has_side_effects=True, vmem_limit_bytes=48 * 1024 * 1024
        ),
    )(x, pair_bins, pair_bins.T, rows_row, tiled)
    out = out.reshape(nrcv * 2, CAP, 2, half, CHUNK).transpose(1, 2, 0, 3, 4)
    return out.reshape(CAP, 2, nrcv * width)


def solution(mesh):
    in_specs = (P(("groups", "src"), None, None, "rcv"), P(("groups", "src"), None), P("groups"))
    out_specs = P(("groups", "src", "rcv"), None, None)
    return jax.shard_map(
        per_device, mesh=mesh, in_specs=in_specs, out_specs=out_specs, check_vma=False
    )
```

time: 218 us -> 39.7 us (0.18)
  other arithmetic: 66.6 us -> 0.19 us
  matrix products: 65.1 us -> 0 us
  waiting for transfers between devices: 35.6 us -> 0 us
  Pallas kernels: 0 us -> 34.2 us
  local copies, waits for them, and re-layouts: 28.4 us -> 5.02 us
  starting transfers between devices: 20 us -> 0 us
    dot_general x22 -> x0, matrix products: 65.1 us -> none  [the longest x10 44.3 us: one_block(): jnp.dot(onehot, corr_im.reshape(-1, width), precision=lax.Precision.HIGHEST)]
    add x11 -> x1, other arithmetic: 51.3 us -> 0.01 us  [per_device(): rows = owners * CAP + jnp.sum((same & earlier).astype(jnp.int32), axis=1)]
    pallas_call x0 -> x1, Pallas kernels: none -> 34.2 us  [per_device(): pl.pallas_call(functools.partial(kernel, dims), out_shape=jax.ShapeDtypeS...]
    ppermute x3 -> x0, waiting for transfers between devices: 21.3 us -> none  [the longest x1 19.8 us: shifted(): return lax.ppermute(block, axis, route)]
    all_to_all x2 -> x0, starting transfers between devices: 15 us -> none  [the longest x1 8.93 us: per_device(): lax.all_to_all(out_counts, ('src', 'rcv'), split_axis=0, concat_axis=0, t...]
    all_to_all x2 -> x0, waiting for transfers between devices: 14.2 us -> none  [the longest x1 14.2 us: per_device(): lax.all_to_all(outgoing, ('src', 'rcv'), split_axis=0, concat_axis=0, til...]
    convert_element_type x12 -> x0, other arithmetic: 11.5 us -> none  [the longest x10 8.59 us: one_block(): own_im = own_im.astype(jnp.float32)]
    dynamic_slice x10 -> x0, local copies, waits for them, and re-layouts: 7.42 us -> none  [per_device(): lax.scan(one_block, init, (own_re_all, own_im_all, labels))]
  transfers between devices with their start and end apart: 5 -> 0, of which waited for: 3 -> 0; matrix products, arithmetic and copies ran while one was open for 65% -> 0% of each run, Pallas kernels for 0% -> 0%
where the time goes in v1:
time: 39.7 us; the launch traced here: 39.5 us
  Pallas kernels  34.2 us (86%)
  local copies, waits for them, and re-layouts  5.02 us (13%)
    pallas_call x1, Pallas kernels, per_device(): pl.pallas_call(functools.partial(kernel, dims), out_shape=jax.ShapeDtypeS...  34.2 us
    reshape x2, local copies, waits for them, and re-layouts, per_device(): x = spectra.reshape(local, windows * 2, chunks, CHUNK).transpose(2, 1, 0, 3)  4.11 us

profile of v1, /device:TPU:0, one launch (start us, length us, event | category | flops | bytes accessed | tf_op | source)
XLA Modules:
  0.0 39.5 jit_solution(1263673631388120663)
XLA Ops:
  0.0 3.4 %reshape.15 = bf16[80,4,8,256]{3,2,1,0:T(8,128)(2,1)S(1)} reshape(bf16[80,2,2,2048]{3,2,1,0:T(2,128)(2,1)} %param.3) | data formatting | bytes 2621440 | tf_op jit(solution)/shard_map/reshape | solution.py:416
  3.4 0.0 copy-start
  3.4 0.0 copy-start.1
  3.4 0.7 %copy.17 = bf16[80,4,8,256]{3,0,1,2:T(8,128)(2,1)S(1)} copy(bf16[80,4,8,256]{3,2,1,0:T(8,128)(2,1)S(1)} %reshape.15) | data formatting | bytes 2621440 | tf_op jit(solution)/shard_map/reshape | solution.py:416
  4.1 0.0 copy-done
  4.2 0.1 copy.12
  4.2 0.0 copy-done.1
  4.3 0.2 convert_reduce_fusion
  4.5 0.1 broadcast_in_dim_tile.3.tiled_ref
  4.5 34.2 %shard_map.37 = f32[4,16,256]{2,1,0:T(8,128)S(1)} custom-call(bf16[8,4,80,256]{3,2,1,0:T(8,128)(2,1)S(1)} %bitcast.7, s32[80,80]{1,0:T(8,128)S(1)} %copy-done, s32[80,80]{1,0:T(8,128)S(1)} %bitcast.8, s32[1,128]{1,0:T(1,128)S(1)} %pad_bitcast_fusion.rows_ref, s32[1,128]{1,0:T(1,128)S(1)} %broadcast_in_dim_tile.3.tiled_ref), custom_call_target="tpu_custom_call" | custom-call | tf_op jit(solution)/shard_map/pallas_call | solution.py:427
  38.8 0.7 %reshape.14 = f32[2,2,4096]{2,1,0:T(2,128)} reshape(f32[2,2,4,4,256]{4,3,2,1,0:T(4,128)S(1)} %copy.13) | data formatting | bytes 131072 | tf_op jit(solution)/shard_map/reshape | solution.py:465
  (5 shorter events, 0.0 us)
Async XLA Ops:
  3.4 0.8 %copy-start = (s32[80,80]{1,0:T(8,128)S(1)}, s32[80,80]{1,0:T(8,128)}, u32[]{:S(2)}) copy-start(s32[80,80]{1,0:T(8,128)} %lab_ref.1) | copy-start | bytes 76804
  3.4 0.9 %copy-start.1 = (s32[16]{0:T(128)S(1)}, s32[16]{0:T(128)}, u32[]{:S(2)}) copy-start(s32[16]{0:T(128)} %param.5) | copy-start | bytes 196

commit v2 on v1

--- a/solution.py
+++ b/solution.py
@@ -34,6 +34,7 @@
     own,
     prod,
     acc,
+    pick,
     send_part,
     recv_part,
     lab_in,
@@ -91,17 +92,22 @@
         buffer[:, EDGE + width :] = zero
 
     def magnitudes(j, carry):
+        at = pl.ds(pl.multiple_of(j * CHUNK, 128), CHUNK)
         for w in range(windows):
             put_magnitude(
-                x_ref[j, 2 * w],
-                x_ref[j, 2 * w + 1],
+                x_ref[2 * w, :, at],
+                x_ref[2 * w + 1, :, at],
                 w * local,
                 pl.multiple_of(EDGE + j * CHUNK, 128),
                 CHUNK,
             )
         return carry
 
-    lax.fori_loop(0, chunks, magnitudes, 0)
+    def inside(j):
+        return jnp.minimum(jnp.maximum(j, 0), chunks - 1)
+
+    for t in range(-1, 2):
+        magnitudes(inside(place(1 - par, t)), 0)
     tall = CHUNK + 2 * EDGE
     k_ids = lax.broadcasted_iota(jnp.int32, (tall, CHUNK), 0) - EDGE
     n_ids = lax.broadcasted_iota(jnp.int32, (tall, CHUNK), 1)
@@ -117,7 +123,8 @@
         for w in range(windows):
             part = inverse[w * local : (w + 1) * local]
             for p in range(2):
-                white[j, 2 * w + p] = (x_ref[j, 2 * w + p].astype(f32) * part).astype(jnp.bfloat16)
+                raw = x_ref[2 * w + p, :, pl.ds(pl.multiple_of(j * CHUNK, 128), CHUNK)]
+                white[j, 2 * w + p] = (raw.astype(f32) * part).astype(jnp.bfloat16)
 
     partner = s + 1 - 2 * par
     beyond = s + 2 - 4 * par
@@ -125,29 +132,29 @@
     back = s - 2 + 4 * par
     has_far = (back >= 0) & (back < nsrc)
 
-    def near_copy(t):
+    def near_copy(t, k):
         return pltpu.make_async_remote_copy(
-            src_ref=white.at[place(1 - par, t)],
-            dst_ref=near.at[t],
-            send_sem=near_send.at[t],
-            recv_sem=near_recv.at[t],
+            src_ref=white.at[place(1 - par, t), k],
+            dst_ref=near.at[t, k],
+            send_sem=near_send.at[t, k],
+            recv_sem=near_recv.at[t, k],
             device_id={"src": partner},
             device_id_type=MESH,
         )
 
-    def far_copy(t):
+    def far_copy(t, k):
         return pltpu.make_async_remote_copy(
-            src_ref=near.at[t],
-            dst_ref=far.at[t],
-            send_sem=far_send.at[t],
-            recv_sem=far_recv.at[t],
+            src_ref=near.at[t, k],
+            dst_ref=far.at[t, k],
+            send_sem=far_send.at[t, k],
+            recv_sem=far_recv.at[t, k],
             device_id={"src": beyond},
             device_id_type=MESH,
         )
 
     halo_copy = pltpu.make_async_remote_copy(
         src_ref=x_ref.at[
-            (1 - r) * (chunks - 1), :, :, pl.ds(pl.multiple_of((1 - r) * (CHUNK - EDGE), 128), EDGE)
+            :, :, pl.ds(pl.multiple_of((1 - r) * (width - EDGE), 128), EDGE)
         ],
         dst_ref=halo,
         send_sem=halo_sems.at[0],
@@ -167,18 +174,25 @@
     whiten(place(1 - par, 0))
     pl.semaphore_wait(barrier, ndev - 1)
     halo_copy.start()
-    near_copy(0).start()
+
+    def send_near(t):
+        for k in range(2 * windows):
+            near_copy(t, k).start()
+
+    send_near(0)
 
     @pl.when(s + 1 < nsrc)
     def _():
         lab_copy.start()
 
     def send_next(t, carry):
+        magnitudes(inside(place(1 - par, t + 1)), 0)
         whiten(place(1 - par, t))
-        near_copy(t).start()
+        send_near(t)
         return carry
 
     lax.fori_loop(1, half - 1, send_next, 0)
+    magnitudes(inside(place(1 - par, half)), 0)
     halo_copy.wait_recv()
     for w in range(windows):
         put_magnitude(
@@ -189,7 +203,7 @@
             EDGE,
         )
     whiten(place(1 - par, half - 1))
-    near_copy(half - 1).start()
+    send_near(half - 1)
 
     labels = lab_ref[...]
     lanes = count_out.shape[1]
@@ -222,6 +236,11 @@
 
     lax.fori_loop(1, nsrc, send_count, 0)
 
+    def keep_magnitude(t, carry):
+        return magnitudes(place(par, t), carry)
+
+    lax.fori_loop(0, half, keep_magnitude, 0)
+
     def keep(t, carry):
         whiten(place(par, t))
         return carry
@@ -240,6 +259,25 @@
             return carry
 
         lax.fori_loop(0, nbins, expand_previous, 0)
+
+    lines = CAP * 2 * half
+    cols = half * 2 * nbins
+    batch = 16
+    row_ids = lax.broadcasted_iota(jnp.int32, (batch * lines, cols), 0)
+    col_ids = lax.broadcasted_iota(jnp.int32, (batch * lines, cols), 1)
+    row_line = lax.rem(row_ids, 2 * half)
+    col_turn = col_ids // (2 * nbins)
+    col_line = lax.rem(col_ids // nbins, 2) * half + r * (half - 1) + col_turn * (1 - 2 * r)
+    same_line = row_line == col_line
+    row_slot = row_ids // (2 * half)
+
+    def prepare(g, carry):
+        chosen = same_line & (tiled_ref[...] == row_slot + g * (batch * CAP))
+        at = pl.ds(pl.multiple_of(g * (batch * lines), 16), batch * lines)
+        pick[at] = jnp.where(chosen, 1.0, 0.0).astype(jnp.bfloat16)
+        return carry
+
+    lax.fori_loop(0, ndev // batch, prepare, 0)
 
     def correlate(which, other, t, first):
         for k in range(2 * windows):
@@ -277,17 +315,19 @@
         lax.fori_loop(0, nbins // group, some, 0)
 
     def near_turn(t, carry):
-        near_copy(t).wait_recv()
-
-        @pl.when(sends_far)
-        def _():
-            far_copy(t).start()
+        for k in range(2 * windows):
+            near_copy(t, k).wait_recv()
+
+            @pl.when(sends_far)
+            def _():
+                far_copy(t, k).start()
 
         correlate(par, near, t, True)
         return carry
 
     def far_turn(t, carry):
-        far_copy(t).wait_recv()
+        for k in range(2 * windows):
+            far_copy(t, k).wait_recv()
         correlate(1 - par, far, t, False)
         return carry
 
@@ -301,48 +341,6 @@
         return carry
 
     lax.fori_loop(0, half, turn, 0)
-
-    @pl.when(has_far)
-    def _():
-        far_turn(half - 1, 0)
-
-    lines = CAP * 2 * half
-    cols = half * 2 * nbins
-    stacked = acc[...].reshape(cols, CHUNK).astype(jnp.bfloat16)
-    batch = 16
-    row_ids = lax.broadcasted_iota(jnp.int32, (batch * lines, cols), 0)
-    col_ids = lax.broadcasted_iota(jnp.int32, (batch * lines, cols), 1)
-    row_line = lax.rem(row_ids, 2 * half)
-    col_turn = col_ids // (2 * nbins)
-    col_line = lax.rem(col_ids // nbins, 2) * half + r * (half - 1) + col_turn * (1 - 2 * r)
-    same_line = row_line == col_line
-    row_slot = row_ids // (2 * half)
-
-    def route(g, carry):
-        pick = same_line & (tiled_ref[...] == row_slot + g * (batch * CAP))
-        at = pl.ds(pl.multiple_of(g * (batch * lines), 16), batch * lines)
-        pick = jnp.where(pick, 1.0, 0.0).astype(jnp.bfloat16)
-        send_part[at] = jnp.dot(pick, stacked, preferred_element_type=f32).astype(jnp.bfloat16)
-        return carry
-
-    lax.fori_loop(0, ndev // batch, route, 0)
-
-    def part_copy(o, slot):
-        return pltpu.make_async_remote_copy(
-            src_ref=send_part.at[pl.ds(pl.multiple_of(o * lines, 16), lines)],
-            dst_ref=recv_part.at[slot],
-            send_sem=part_send.at[o],
-            recv_sem=part_recv.at[slot],
-            device_id={"src": o // nrcv, "rcv": lax.rem(o, nrcv)},
-            device_id_type=MESH,
-        )
-
-    def send_one(k, carry):
-        part_copy(lax.rem(me + k, ndev), me).start()
-        return carry
-
-    lax.fori_loop(1, ndev, send_one, 0)
-    recv_part[me] = send_part[pl.ds(pl.multiple_of(me * lines, 16), lines)]
 
     def take_count(k, carry):
         o = lax.rem(s + k, nsrc)
@@ -360,6 +358,36 @@
     for c in range(CAP):
         norm = jnp.where(line_ids == c, jnp.sqrt(jnp.maximum(mine[c], 1.0)), norm)
 
+    @pl.when(has_far)
+    def _():
+        far_turn(half - 1, 0)
+
+    stacked = acc[...].reshape(cols, CHUNK).astype(jnp.bfloat16)
+
+    def route(g, carry):
+        at = pl.ds(pl.multiple_of(g * (batch * lines), 16), batch * lines)
+        send_part[at] = jnp.dot(pick[at], stacked, preferred_element_type=f32).astype(jnp.bfloat16)
+        return carry
+
+    lax.fori_loop(0, ndev // batch, route, 0)
+
+    def part_copy(o, slot):
+        return pltpu.make_async_remote_copy(
+            src_ref=send_part.at[pl.ds(pl.multiple_of(o * lines, 16), lines)],
+            dst_ref=recv_part.at[slot],
+            send_sem=part_send.at[o],
+            recv_sem=part_recv.at[slot],
+            device_id={"src": o // nrcv, "rcv": lax.rem(o, nrcv)},
+            device_id_type=MESH,
+        )
+
+    def send_one(k, carry):
+        part_copy(lax.rem(me + k, ndev), me).start()
+        return carry
+
+    lax.fori_loop(1, ndev, send_one, 0)
+    recv_part[me] = send_part[pl.ds(pl.multiple_of(me * lines, 16), lines)]
+
     def take_part(k, carry):
         o = lax.rem(me + k, ndev)
         part_copy(o, o).wait_recv()
@@ -376,12 +404,14 @@
             out_ref[rr * 2 + pp] = total / norm
 
     for t in range(half):
-        near_copy(t).wait_send()
+        for k in range(2 * windows):
+            near_copy(t, k).wait_send()
 
     @pl.when(sends_far)
     def _():
         for t in range(half):
-            far_copy(t).wait_send()
+            for k in range(2 * windows):
+                far_copy(t, k).wait_send()
 
     halo_copy.wait_send()
 
@@ -413,7 +443,7 @@
     lines = CAP * 2 * half
     lanes = -(-nbins // 128) * 128
     group = 8
-    x = spectra.reshape(local, windows * 2, chunks, CHUNK).transpose(2, 1, 0, 3)
+    x = spectra.reshape(local, windows * 2, width).transpose(1, 0, 2)
     bin_ids = jnp.arange(nbins, dtype=jnp.int32)
     same = owners[:, None] == owners[None, :]
     earlier = bin_ids[None, :] < bin_ids[:, None]
@@ -441,15 +471,16 @@
             pltpu.VMEM((2 * windows, local, CHUNK), f32),
             pltpu.VMEM((2 * windows, group * local, CHUNK), f32),
             pltpu.VMEM((half, 2, nbins, CHUNK), f32),
+            pltpu.VMEM((ndev * lines, half * 2 * nbins), bf16),
             pltpu.VMEM((ndev * lines, CHUNK), bf16),
             pltpu.VMEM((ndev, lines, CHUNK), bf16),
             pltpu.VMEM((local, local), jnp.int32),
             pltpu.VMEM((8, lanes), f32),
             pltpu.VMEM((nsrc, 8, lanes), f32),
-            dma((half,)),
-            dma((half,)),
-            dma((half,)),
-            dma((half,)),
+            dma((half, 2 * windows)),
+            dma((half, 2 * windows)),
+            dma((half, 2 * windows)),
+            dma((half, 2 * windows)),
             dma((2,)),
             dma((2,)),
             dma((nsrc,)),

time: 39.7 us -> 40.3 us (1.015)
  other arithmetic: 0.19 us -> 1.57 us
  local copies, waits for them, and re-layouts: 5.02 us -> 3.72 us
  Pallas kernels: 34.2 us -> 34.7 us
    reshape x2 -> x0, local copies, waits for them, and re-layouts: 4.11 us -> none  [per_device(): x = spectra.reshape(local, windows * 2, chunks, CHUNK).transpose(2, 1, 0, 3)]
    unnamed x5 -> x4, local copies, waits for them, and re-layouts: 0.1 us -> 2.91 us
    reduce_sum x1, other arithmetic: 0.18 us -> 0.91 us  [per_device(): rows = owners * CAP + jnp.sum((same & earlier).astype(jnp.int32), axis=1)]
    add x1, other arithmetic: 0.01 us -> 0.66 us  [per_device(): rows = owners * CAP + jnp.sum((same & earlier).astype(jnp.int32), axis=1)]
    pallas_call x1, Pallas kernels: 34.2 us -> 34.7 us  [per_device(): pl.pallas_call(functools.partial(kernel, dims), out_shape=jax.ShapeDtypeS...]
where the time goes in v2:
time: 40.3 us; the launch traced here: 40.1 us
  Pallas kernels  34.7 us (86%)
  local copies, waits for them, and re-layouts  3.72 us (9%)
  other arithmetic  1.57 us (4%)
    pallas_call x1, Pallas kernels, per_device(): pl.pallas_call(functools.partial(kernel, dims), out_shape=jax.ShapeDtypeS...  34.7 us
    unnamed x4, local copies, waits for them, and re-layouts  2.91 us
    reduce_sum x1, other arithmetic, per_device(): rows = owners * CAP + jnp.sum((same & earlier).astype(jnp.int32), axis=1)  0.91 us

profile of v2, /device:TPU:0, one launch (start us, length us, event | category | flops | bytes accessed | tf_op | source)
XLA Modules:
  0.0 40.1 jit_solution(13028187845178573630)
XLA Ops:
  0.0 0.9 %convert_reduce_fusion = s32[16]{0:T(128)S(1)} fusion(s32[16]{0:T(128)} %param.5), kind=kLoop, calls=%fused_computation | loop fusion | flops 1264 | bytes 128 | tf_op jit(solution)/shard_map/reduce_sum | solution.py:450
  0.9 0.7 %multiply_add_fusion = s32[16]{0:T(128)S(1)} fusion(s32[16]{0:T(128)S(1)} %convert_reduce_fusion, s32[16]{0:T(128)} %param.5), kind=kLoop, calls=%fused_computation.4 | loop fusion | flops 32 | bytes 192 | tf_op jit(solution)/shard_map/add | solution.py:450
  1.6 0.1 broadcast_in_dim_tile.3.tiled_ref
  1.7 0.9 %copy.8 = s32[80,80]{0,1:T(8,128)S(1)} copy(s32[80,80]{1,0:T(8,128)} %lab_ref.1) | data formatting | bytes 51200 | tf_op args[1]
  2.5 0.0 copy-start
  2.5 2.1 %copy.7 = bf16[80,2,2,2048]{3,0,2,1:T(8,128)(2,1)S(1)} copy(bf16[80,2,2,2048]{3,2,1,0:T(2,128)(2,1)} %param.3) | data formatting | bytes 2621440 | tf_op args[0]
  4.6 0.0 copy-done
  4.6 34.7 %shard_map.37 = f32[4,16,256]{2,1,0:T(8,128)S(1)} custom-call(bf16[4,80,2048]{2,1,0:T(8,128)(2,1)S(1)} %bitcast.7, s32[80,80]{1,0:T(8,128)S(1)} %copy-done, s32[80,80]{1,0:T(8,128)S(1)} %bitcast.8, s32[1,128]{1,0:T(1,128)S(1)} %pad_bitcast_fusion.rows_ref, s32[1,128]{1,0:T(1,128)S(1)} %broadcast_in_dim_tile.3.tiled_ref), custom_call_target="tpu_custom_call" | custom-call | tf_op jit(solution)/shard_map/pallas_call | solution.py:457
  39.4 0.7 %reshape.14 = f32[2,2,4096]{2,1,0:T(2,128)} reshape(f32[2,2,4,4,256]{4,3,2,1,0:T(4,128)S(1)} %copy.9) | data formatting | bytes 131072 | tf_op jit(solution)/shard_map/reshape | solution.py:496
  (4 shorter events, 0.0 us)
Async XLA Ops:
  2.5 2.1 %copy-start = (s32[80,80]{1,0:T(8,128)S(1)}, s32[80,80]{1,0:T(8,128)}, u32[]{:S(2)}) copy-start(s32[80,80]{1,0:T(8,128)} %lab_ref.1) | copy-start | bytes 76804

commit v3 on v2

--- a/solution.py
+++ b/solution.py
@@ -19,9 +19,7 @@
     dims,
     x_ref,
     lab_ref,
-    labt_ref,
-    rows_ref,
-    tiled_ref,
+    owners_ref,
     out_ref,
     white,
     near,
@@ -163,7 +161,7 @@
         device_id_type=MESH,
     )
     lab_copy = pltpu.make_async_remote_copy(
-        src_ref=labt_ref,
+        src_ref=lab_ref,
         dst_ref=lab_in,
         send_sem=lab_sems.at[0],
         recv_sem=lab_sems.at[1],
@@ -236,21 +234,34 @@
 
     lax.fori_loop(1, nsrc, send_count, 0)
 
+    def relay(t, k):
+        near_copy(t, k).wait_recv()
+
+        @pl.when(sends_far)
+        def _():
+            far_copy(t, k).start()
+
+    relay(0, 0)
+
     def keep_magnitude(t, carry):
         return magnitudes(place(par, t), carry)
 
     lax.fori_loop(0, half, keep_magnitude, 0)
 
+    relay(0, 1)
+
     def keep(t, carry):
         whiten(place(par, t))
         return carry
 
     lax.fori_loop(0, half, keep, 0)
+
+    relay(0, 2)
 
     @pl.when(s > 0)
     def _():
         lab_copy.wait_recv()
-        previous = lab_in[...]
+        previous = jnp.transpose(lab_in[...].astype(f32)).astype(jnp.int32)
 
         def expand_previous(b, carry):
             onehot[1, pl.ds(pl.multiple_of(b * local, 16), local), :] = jnp.where(
@@ -260,6 +271,27 @@
 
         lax.fori_loop(0, nbins, expand_previous, 0)
 
+    relay(0, 3)
+    owned = owners_ref[...]
+    b_rows = lax.broadcasted_iota(jnp.int32, (nbins, nbins), 0)
+    b_cols = lax.broadcasted_iota(jnp.int32, (nbins, nbins), 1)
+    column = jnp.sum(jnp.where(b_rows == b_cols, owned, 0).astype(f32), axis=1, keepdims=True)
+    earlier = jnp.where((column.astype(jnp.int32) == owned) & (b_rows < b_cols), 1.0, 0.0)
+    slots = jnp.sum(earlier.astype(f32), axis=0, keepdims=True)
+    rows_row = owned.astype(f32) * CAP + slots
+    spread = jnp.where(
+        lax.broadcasted_iota(jnp.int32, (nbins, 2 * half * nbins), 0)
+        == lax.rem(lax.broadcasted_iota(jnp.int32, (nbins, 2 * half * nbins), 1), nbins),
+        1.0,
+        0.0,
+    ).astype(f32)
+    tiled = jnp.dot(
+        jnp.broadcast_to(rows_row, (8, nbins)),
+        spread,
+        precision=lax.Precision.HIGHEST,
+        preferred_element_type=f32,
+    )[0:1].astype(jnp.int32)
+    rows_row = rows_row.astype(jnp.int32)
     lines = CAP * 2 * half
     cols = half * 2 * nbins
     batch = 16
@@ -272,7 +304,7 @@
     row_slot = row_ids // (2 * half)
 
     def prepare(g, carry):
-        chosen = same_line & (tiled_ref[...] == row_slot + g * (batch * CAP))
+        chosen = same_line & (tiled == row_slot + g * (batch * CAP))
         at = pl.ds(pl.multiple_of(g * (batch * lines), 16), batch * lines)
         pick[at] = jnp.where(chosen, 1.0, 0.0).astype(jnp.bfloat16)
         return carry
@@ -314,33 +346,29 @@
 
         lax.fori_loop(0, nbins // group, some, 0)
 
-    def near_turn(t, carry):
-        for k in range(2 * windows):
-            near_copy(t, k).wait_recv()
-
-            @pl.when(sends_far)
-            def _():
-                far_copy(t, k).start()
-
+    def near_turn(t):
         correlate(par, near, t, True)
-        return carry
-
-    def far_turn(t, carry):
+
+    def far_turn(t):
         for k in range(2 * windows):
             far_copy(t, k).wait_recv()
         correlate(1 - par, far, t, False)
-        return carry
 
     def turn(t, carry):
-        near_turn(t, 0)
-
-        @pl.when((t > 0) & has_far)
+        relay(t, 0)
+        near_turn(t - 1)
+        for k in range(1, 2 * windows - 1):
+            relay(t, k)
+
+        @pl.when(has_far)
         def _():
-            far_turn(t - 1, 0)
-
-        return carry
-
-    lax.fori_loop(0, half, turn, 0)
+            far_turn(t - 1)
+
+        relay(t, 2 * windows - 1)
+        return carry
+
+    lax.fori_loop(1, half, turn, 0)
+    near_turn(half - 1)
 
     def take_count(k, carry):
         o = lax.rem(s + k, nsrc)
@@ -348,9 +376,9 @@
         return carry
 
     lax.fori_loop(1, nsrc, take_count, 0)
-    counts = jnp.sum(count_in[...], axis=0)[0:1]
+    counts = jnp.sum(count_in[...], axis=0)[0:1, :nbins]
     mine = [
-        jnp.sum(jnp.where(rows_ref[...] == me * CAP + c, counts, 0.0), axis=1, keepdims=True)
+        jnp.sum(jnp.where(rows_row == me * CAP + c, counts, 0.0), axis=1, keepdims=True)
         for c in range(CAP)
     ]
     line_ids = lax.broadcasted_iota(jnp.int32, (lines, 1), 0) // (2 * half)
@@ -360,7 +388,7 @@
 
     @pl.when(has_far)
     def _():
-        far_turn(half - 1, 0)
+        far_turn(half - 1)
 
     stacked = acc[...].reshape(cols, CHUNK).astype(jnp.bfloat16)
 
@@ -444,12 +472,6 @@
     lanes = -(-nbins // 128) * 128
     group = 8
     x = spectra.reshape(local, windows * 2, width).transpose(1, 0, 2)
-    bin_ids = jnp.arange(nbins, dtype=jnp.int32)
-    same = owners[:, None] == owners[None, :]
-    earlier = bin_ids[None, :] < bin_ids[:, None]
-    rows = owners * CAP + jnp.sum((same & earlier).astype(jnp.int32), axis=1)
-    rows_row = jnp.pad(rows, (0, lanes - nbins), constant_values=-1)[None]
-    tiled = jnp.tile(rows, 2 * half)[None]
     dims = (nsrc, nrcv, nbins, local, windows, chunks, group)
     bf16, f32 = jnp.bfloat16, jnp.float32
     dma = pltpu.SemaphoreType.DMA
@@ -457,7 +479,7 @@
     out = pl.pallas_call(
         functools.partial(kernel, dims),
         out_shape=jax.ShapeDtypeStruct((2 * nrcv, lines, CHUNK), f32),
-        in_specs=[vmem] * 5,
+        in_specs=[vmem] * 3,
         out_specs=vmem,
         scratch_shapes=[
             pltpu.VMEM((chunks, 2 * windows, local, CHUNK), bf16),
@@ -491,7 +513,7 @@
         compiler_params=pltpu.CompilerParams(
             collective_id=0, has_side_effects=True, vmem_limit_bytes=48 * 1024 * 1024
         ),
-    )(x, pair_bins, pair_bins.T, rows_row, tiled)
+    )(x, pair_bins, owners[None])
     out = out.reshape(nrcv * 2, CAP, 2, half, CHUNK).transpose(1, 2, 0, 3, 4)
     return out.reshape(CAP, 2, nrcv * width)
 

time: 40.3 us -> 37.7 us (0.935)
  other arithmetic: 1.57 us -> 0 us
  local copies, waits for them, and re-layouts: 3.72 us -> 2.77 us
    reduce_sum x1 -> x0, other arithmetic: 0.91 us -> none  [per_device(): rows = owners * CAP + jnp.sum((same & earlier).astype(jnp.int32), axis=1)]
    unnamed x4 -> x5, local copies, waits for them, and re-layouts: 2.91 us -> 2.05 us
    add x1 -> x0, other arithmetic: 0.66 us -> none  [per_device(): rows = owners * CAP + jnp.sum((same & earlier).astype(jnp.int32), axis=1)]
where the time goes in v3:
time: 37.7 us; the launch traced here: 37.6 us
  Pallas kernels  34.8 us (92%)
  local copies, waits for them, and re-layouts  2.77 us (7%)
    pallas_call x1, Pallas kernels, per_device(): pl.pallas_call(functools.partial(kernel, dims), out_shape=jax.ShapeDtypeS...  34.8 us
    unnamed x5, local copies, waits for them, and re-layouts  2.05 us

profile of v3, /device:TPU:0, one launch (start us, length us, event | category | flops | bytes accessed | tf_op | source)
XLA Modules:
  0.0 37.6 jit_solution(5548535624180785530)
XLA Ops:
  0.0 0.0 copy-start
  0.0 0.0 copy-start.1
  0.0 2.0 %copy.4 = bf16[80,2,2,2048]{3,0,2,1:T(8,128)(2,1)S(1)} copy(bf16[80,2,2,2048]{3,2,1,0:T(2,128)(2,1)} %param.3) | data formatting | bytes 2621440 | tf_op args[0]
  2.0 0.0 copy-done
  2.1 0.0 copy-done.1
  2.1 34.8 %shard_map.37 = f32[4,16,256]{2,1,0:T(8,128)S(1)} custom-call(bf16[4,80,2048]{2,1,0:T(8,128)(2,1)S(1)} %bitcast.5, s32[80,80]{1,0:T(8,128)S(1)} %copy-done, s32[1,16]{1,0:T(1,128)S(1)} %bitcast.6), custom_call_target="tpu_custom_call" | custom-call | tf_op jit(solution)/shard_map/pallas_call | solution.py:479
  36.9 0.7 %reshape.11 = f32[2,2,4096]{2,1,0:T(2,128)} reshape(f32[2,2,4,4,256]{4,3,2,1,0:T(4,128)S(1)} %copy.5) | data formatting | bytes 131072 | tf_op jit(solution)/shard_map/reshape | solution.py:518
  (2 shorter events, 0.0 us)
Async XLA Ops:
  0.0 2.1 %copy-start = (s32[80,80]{1,0:T(8,128)S(1)}, s32[80,80]{1,0:T(8,128)}, u32[]{:S(2)}) copy-start(s32[80,80]{1,0:T(8,128)} %lab_ref.1) | copy-start | bytes 76804
  0.0 2.1 %copy-start.1 = (s32[16]{0:T(128)S(1)}, s32[16]{0:T(128)}, u32[]{:S(2)}) copy-start(s32[16]{0:T(128)} %param.5) | copy-start | bytes 196

commit v4 on v3

--- a/solution.py
+++ b/solution.py
@@ -1,4 +1,5 @@
 import functools
+import math
 
 import jax
 import jax.numpy as jnp
@@ -35,6 +36,7 @@
     pick,
     send_part,
     recv_part,
+    lab_out,
     lab_in,
     count_out,
     count_in,
@@ -161,7 +163,7 @@
         device_id_type=MESH,
     )
     lab_copy = pltpu.make_async_remote_copy(
-        src_ref=lab_ref,
+        src_ref=lab_out,
         dst_ref=lab_in,
         send_sem=lab_sems.at[0],
         recv_sem=lab_sems.at[1],
@@ -169,6 +171,7 @@
         device_id_type=MESH,
     )
 
+    lab_out[...] = lab_ref[...].astype(f32).astype(jnp.bfloat16)
     whiten(place(1 - par, 0))
     pl.semaphore_wait(barrier, ndev - 1)
     halo_copy.start()
@@ -205,7 +208,7 @@
 
     labels = lab_ref[...]
     lanes = count_out.shape[1]
-    lane_ids = lax.broadcasted_iota(jnp.int32, (8, lanes), 1)
+    lane_ids = lax.broadcasted_iota(jnp.int32, (1, lanes), 1)
     valid = (s + 1 < nsrc).astype(f32)
 
     def expand(b, counted):
@@ -214,7 +217,7 @@
         found = jnp.sum(jnp.sum(hits, axis=0, keepdims=True), axis=1, keepdims=True)
         return counted + jnp.where(lane_ids == b, found, 0.0)
 
-    counted = lax.fori_loop(0, nbins, expand, jnp.zeros((8, lanes), f32)) * valid
+    counted = lax.fori_loop(0, nbins, expand, jnp.zeros((1, lanes), f32)) * valid
     count_out[...] = counted
     count_in[s] = counted
 
@@ -470,7 +473,7 @@
     half = chunks // 2
     lines = CAP * 2 * half
     lanes = -(-nbins // 128) * 128
-    group = 8
+    group = math.gcd(nbins, 16)
     x = spectra.reshape(local, windows * 2, width).transpose(1, 0, 2)
     dims = (nsrc, nrcv, nbins, local, windows, chunks, group)
     bf16, f32 = jnp.bfloat16, jnp.float32
@@ -496,9 +499,10 @@
             pltpu.VMEM((ndev * lines, half * 2 * nbins), bf16),
             pltpu.VMEM((ndev * lines, CHUNK), bf16),
             pltpu.VMEM((ndev, lines, CHUNK), bf16),
-            pltpu.VMEM((local, local), jnp.int32),
-            pltpu.VMEM((8, lanes), f32),
-            pltpu.VMEM((nsrc, 8, lanes), f32),
+            pltpu.VMEM((local, local), bf16),
+            pltpu.VMEM((local, local), bf16),
+            pltpu.VMEM((1, lanes), f32),
+            pltpu.VMEM((nsrc, 1, lanes), f32),
             dma((half, 2 * windows)),
             dma((half, 2 * windows)),
             dma((half, 2 * windows)),

time: 37.7 us -> 36.9 us (0.979)
  Pallas kernels: 34.8 us -> 33.9 us
    pallas_call x1, Pallas kernels: 34.8 us -> 33.9 us  [per_device(): pl.pallas_call(functools.partial(kernel, dims), out_shape=jax.ShapeDtypeS...]
where the time goes in v4:
time: 36.9 us; the launch traced here: 36.7 us
  Pallas kernels  33.9 us (92%)
  local copies, waits for them, and re-layouts  2.77 us (8%)
    pallas_call x1, Pallas kernels, per_device(): pl.pallas_call(functools.partial(kernel, dims), out_shape=jax.ShapeDtypeS...  33.9 us
    unnamed x5, local copies, waits for them, and re-layouts  2.05 us

profile of v4, /device:TPU:0, one launch (start us, length us, event | category | flops | bytes accessed | tf_op | source)
XLA Modules:
  0.0 36.7 jit_solution(4135968056207618167)
XLA Ops:
  0.0 0.0 copy-start
  0.0 0.0 copy-start.1
  0.0 2.0 %copy.4 = bf16[80,2,2,2048]{3,0,2,1:T(8,128)(2,1)S(1)} copy(bf16[80,2,2,2048]{3,2,1,0:T(2,128)(2,1)} %param.3) | data formatting | bytes 2621440 | tf_op args[0]
  2.0 0.0 copy-done
  2.1 0.0 copy-done.1
  2.1 33.9 %shard_map.37 = f32[4,16,256]{2,1,0:T(8,128)S(1)} custom-call(bf16[4,80,2048]{2,1,0:T(8,128)(2,1)S(1)} %bitcast.5, s32[80,80]{1,0:T(8,128)S(1)} %copy-done, s32[1,16]{1,0:T(1,128)S(1)} %bitcast.6), custom_call_target="tpu_custom_call" | custom-call | tf_op jit(solution)/shard_map/pallas_call | solution.py:482
  36.1 0.7 %reshape.11 = f32[2,2,4096]{2,1,0:T(2,128)} reshape(f32[2,2,4,4,256]{4,3,2,1,0:T(4,128)S(1)} %copy.5) | data formatting | bytes 131072 | tf_op jit(solution)/shard_map/reshape | solution.py:522
  (2 shorter events, 0.0 us)
Async XLA Ops:
  0.0 2.1 %copy-start = (s32[80,80]{1,0:T(8,128)S(1)}, s32[80,80]{1,0:T(8,128)}, u32[]{:S(2)}) copy-start(s32[80,80]{1,0:T(8,128)} %lab_ref.1) | copy-start | bytes 76804
  0.0 2.1 %copy-start.1 = (s32[16]{0:T(128)S(1)}, s32[16]{0:T(128)}, u32[]{:S(2)}) copy-start(s32[16]{0:T(128)} %param.5) | copy-start | bytes 196
